TPU v7x, 128 devices: a whole 4x4x4 slice. The times are simulated.
128 devices in a mesh: dp: 32 (over y_lo, z, x), mp: 4 (over y_hi, core).
Axes of the slice: x: 4, y: 4 (y_hi: 2, y_lo: 2; y = y_hi * 2 + y_lo), z: 4, core: 2. Of those that a mesh axis runs over, the one named last changes fastest.
Arguments:
- layer_inputs: bfloat16 [16384, 8192], P('dp', 'mp'), may hold values from -54 to 54
- out_grads: bfloat16 [16384, 28672], P('dp', 'mp'), may hold values from -54 to 54
- loss_mask: int32 [16384], P('dp'), may hold values 0 or 1
- start_in: int32 [64, 8192], P(None, 'mp'), may hold values from -127 to 127
- start_out: int32 [64, 28672], P(None, 'mp'), may hold values from -127 to 127
Outputs:
- features: float32 [64, 4096], P('dp', 'mp')
- basis_in: float32 [64, 8192], P(None, 'mp')
- basis_out: float32 [64, 28672], P(None, 'mp')
All inputs are finite; a program needn't handle non-finite values. No bound on the sum of `loss_mask` on one device may be relied on, other than what follows from the above.
Results may differ from a plain program's by a relative error of at most 0.0065.
Values may be sent and summed in bfloat16 or wider, within the bound.
No kernel may reach another device: no remote copies, remote signals or barrier semaphores. Data moves between devices by JAX's collectives and lax.ppermute only.
A program may use at most 64 MiB of HBM per device.

v0:
```python
import jax
import jax.numpy as jnp
from jax import lax
from jax.sharding import PartitionSpec as P

ITERS = 2
LEN = 256


def coords_of(data, basis_half):
    return lax.dot_general(
        data, basis_half, (((1,), (1,)), ((), ())), preferred_element_type=jnp.float32
    )


def image_of(coords_half, data):
    return lax.dot_general(
        coords_half, data, (((0,), (0,)), ((), ())), preferred_element_type=jnp.float32
    )


def gram_of(image):
    return jnp.dot(image, image.T, precision=lax.Precision.HIGHEST)


def normalize(gram, image):
    lower = jnp.linalg.cholesky(gram)
    return jax.scipy.linalg.solve_triangular(lower, image, lower=True)


def shards(layer_inputs, out_grads, loss_mask, start_in, start_out):
    keep = loss_mask.astype(jnp.float32)[:, None]
    basis_in = start_in.astype(jnp.float32) / 128.0
    basis_out = start_out.astype(jnp.float32) / 128.0
    half_in = basis_in.astype(jnp.bfloat16)
    half_out = basis_out.astype(jnp.bfloat16)
    for step in range(ITERS):
        in_coords = coords_of(layer_inputs, half_in)
        out_coords = coords_of(out_grads, half_out) * keep
        in_coords, out_coords = lax.psum((in_coords, out_coords), "mp")
        in_image = image_of(in_coords.astype(jnp.bfloat16), layer_inputs)
        out_image = image_of(out_coords.astype(jnp.bfloat16), out_grads)
        out_owned = lax.psum_scatter(out_image, "dp", scatter_dimension=1, tiled=True)
        in_whole = lax.psum(in_image, "dp")
        gram_in = lax.psum(gram_of(in_whole), "mp")
        gram_out = lax.psum(gram_of(out_owned), ("dp", "mp"))
        new_in = normalize(gram_in, in_whole)
        new_out = normalize(gram_out, out_owned)
        if step + 1 < ITERS:
            half_in = new_in.astype(jnp.bfloat16)
            half_out = lax.all_gather(new_out.astype(jnp.bfloat16), "dp", axis=1, tiled=True)
        else:
            basis_in = new_in
            basis_out = lax.all_gather(new_out, "dp", axis=1, tiled=True)
    half_in = basis_in.astype(jnp.bfloat16)
    half_out = basis_out.astype(jnp.bfloat16)
    proj_in = coords_of(layer_inputs, half_in)
    proj_out = coords_of(out_grads, half_out) * keep
    rank = half_in.shape[0]
    seq_count = layer_inputs.shape[0] // LEN
    proj_in, proj_out = lax.psum((proj_in, proj_out), "mp")
    block = rank // lax.axis_size("mp")
    first = lax.axis_index("mp") * block
    part_in = lax.dynamic_slice_in_dim(proj_in.astype(jnp.bfloat16), first, block, 1)
    seq_in = part_in.reshape(seq_count, LEN, block)
    seq_out = proj_out.astype(jnp.bfloat16).reshape(seq_count, LEN, rank)
    summed = jnp.einsum("sti,stj->sij", seq_in, seq_out, preferred_element_type=jnp.float32) / LEN
    features = summed.reshape(seq_count, block * rank)
    return (features, basis_in, basis_out)


def solution(mesh):
    in_specs = (P("dp", "mp"), P("dp", "mp"), P("dp"), P(None, "mp"), P(None, "mp"))
    out_specs = (P("dp", "mp"), P(None, "mp"), P(None, "mp"))
    return jax.shard_map(shards, mesh=mesh, in_specs=in_specs, out_specs=out_specs, check_vma=False)
```

profile of v0, /device:TPU:1, one launch (start us, length us, event | category | flops | bytes accessed | tf_op | source)
XLA Modules:
  0.0 1492.7 jit_solution(5499521624738872316)
XLA Ops:
  10.6 15.8 %all-reduce.13 = bf16[512,64]{0,1:T(8,128)(2,1)S(1)} all-reduce(f32[512,64]{0,1:T(8,128)S(1)} %convolution_bitcast_fusion.4), channel_id=1, replica_groups=mesh['dp'=32,'mp'=4] {'mp'}, use_global_device_ids=true, to_apply=%region_0.0 | all-reduce | flops 32768 | bytes 196608 | tf_op jit(solution)/shard_map/psum | solution.py:40
  27.7 6.0 fusion.2
  33.7 285.4 %all-reduce.10.cloned.1.call-done = f32[64,2048]{1,0:T(8,128)} async-done(((f32[64,2048]{1,0:T(8,128)}), f32[64,2048]{1,0:T(8,128)}) %all-reduce.10.cloned.1.call-update) | async-done | bytes 524304 | tf_op jit(solution)/shard_map/psum | solution.py:44
  320.9 34.3 %psum.86 = f32[64,64]{0,1:T(8,128)S(1)} all-reduce(f32[64,64]{0,1:T(8,128)S(1)} %fusion.41), channel_id=1, replica_groups=mesh['dp'=32,'mp'=4] {'mp'}, use_global_device_ids=true, to_apply=%region_2.0 | all-reduce | flops 4096 | bytes 32768 | tf_op jit(solution)/shard_map/psum | solution.py:45
  355.3 5.8 cholesky.74
  369.8 16.8 %all-reduce.14 = (bf16[512,64]{0,1:T(8,128)(2,1)S(1)}, bf16[512,64]{0,1:T(8,128)(2,1)S(1)}) all-reduce(f32[512,64]{0,1:T(8,128)S(1)} %fusion.2, f32[512,64]{0,1:T(8,128)S(1)} %convolution_bitcast_fusion.3), channel_id=1, replica_groups=mesh['dp'=32,'mp'=4] {'mp'}, use_global_device_ids=true, to_apply=%region_9.12 | all-reduce | flops 65536 | bytes 393216 | tf_op jit(solution)/shard_map/psum | solution.py:40
  388.0 7.9 convolution_bitcast_fusion.1
  395.9 281.3 %all-reduce.12.cloned.1.call-done = f32[64,2048]{1,0:T(8,128)} async-done(((f32[64,2048]{1,0:T(8,128)}), f32[64,2048]{1,0:T(8,128)}) %all-reduce.12.cloned.1.call-update) | async-done | bytes 524304 | tf_op jit(solution)/shard_map/psum | solution.py:44
  679.0 167.0 %reduce-scatter.7.cloned.1.call-done = f32[224,64]{1,0:T(8,128)} async-done(((f32[7168,64]{1,0:T(8,128)}), f32[224,64]{1,0:T(8,128)}) %reduce-scatter.7.cloned.1.call-update) | async-done | bytes 57360
  847.4 86.2 %psum.92 = f32[64,64]{0,1:T(8,128)S(1)} all-reduce(f32[64,64]{0,1:T(8,128)S(1)} %fusion.11), channel_id=1, replica_groups=mesh['dp'=32,'mp'=4] {'dp','mp'}, use_global_device_ids=true, to_apply=%region_11.14 | all-reduce | flops 4096 | bytes 32768 | tf_op jit(solution)/shard_map/psum | solution.py:46
  933.6 5.8 cholesky.96
  947.0 69.9 %all-gather = bf16[32,224,64]{1,2,0:T(8,128)(2,1)S(1)} all-gather(bf16[1,224,64]{1,2,0:T(8,128)(2,1)S(1)} %fusion.3), channel_id=1, replica_groups=mesh['dp'=32,'mp'=4] {'dp'}, dimensions={0}, use_global_device_ids=true | all-gather | bytes 946176 | tf_op jit(solution)/shard_map/all_gather | solution.py:51
  1020.2 5.7 fusion.1
  1026.0 28.4 %all-reduce.15 = (bf16[512,64]{0,1:T(8,128)(2,1)S(1)}, f32[64,64]{0,1:T(8,128)S(1)}) all-reduce(f32[512,64]{0,1:T(8,128)S(1)} %fusion.1, f32[64,64]{0,1:T(8,128)S(1)} %fusion.42), channel_id=1, replica_groups=mesh['dp'=32,'mp'=4] {'mp'}, use_global_device_ids=true, to_apply=%region_12.0 | all-reduce | flops 36864 | bytes 229376 | tf_op jit(solution)/shard_map/psum | solution.py:40
  1054.4 7.9 convolution_bitcast_fusion
  1062.4 140.7 %reduce-scatter.9.cloned.1.call-done = f32[224,64]{1,0:T(8,128)} async-done(((f32[7168,64]{1,0:T(8,128)}), f32[224,64]{1,0:T(8,128)}) %reduce-scatter.9.cloned.1.call-update) | async-done | bytes 57360
  1204.4 86.6 %psum.94 = f32[64,64]{0,1:T(8,128)S(1)} all-reduce(f32[64,64]{0,1:T(8,128)S(1)} %fusion.8), channel_id=1, replica_groups=mesh['dp'=32,'mp'=4] {'dp','mp'}, use_global_device_ids=true, to_apply=%region_14.18 | all-reduce | flops 4096 | bytes 32768 | tf_op jit(solution)/shard_map/psum | solution.py:46
  1291.1 5.8 cholesky.107
  1298.3 4.9 custom-call.13
  1305.2 5.8 cholesky.85
  1312.4 4.9 custom-call.11
  1318.7 114.7 %all-gather.4.cloned.1.call-done = f32[32,224,64]{1,2,0:T(8,128)} async-done(((f32[1,224,64]{1,2,0:T(8,128)}), f32[32,224,64]{1,2,0:T(8,128)}) %all-gather.4.cloned.1.call-update) | async-done | bytes 1835024 | tf_op jit(solution)/shard_map/all_gather | solution.py:54
  1441.0 6.0 fusion
  1446.9 38.4 %all-reduce.16 = (bf16[512,64]{0,1:T(8,128)(2,1)S(1)}, bf16[512,64]{0,1:T(8,128)(2,1)S(1)}) all-reduce(f32[512,64]{0,1:T(8,128)S(1)} %fusion, f32[512,64]{0,1:T(8,128)S(1)} %convolution_bitcast_fusion.2), channel_id=1, replica_groups=mesh['dp'=32,'mp'=4] {'mp'}, use_global_device_ids=true, to_apply=%region_15.19 | all-reduce | flops 65536 | bytes 393216 | tf_op jit(solution)/shard_map/psum | solution.py:61
  (61 shorter events, 46.5 us)
Async XLA Ops:
  7.2 1.6 copy-start
  7.2 312.0 %all-reduce.10.cloned.1.call-start = ((), (), s32[]{:S(2)}) async-start(), calls=%async_computation.2 | async-start | bytes 1048576 | tf_op jit(solution)/shard_map/psum | solution.py:44
  10.6 17.1 %copy-start.3 = (s32[512]{0:T(512)S(1)}, s32[512]{0:T(512)}, u32[]{:S(2)}) copy-start(s32[512]{0:T(512)} %param.12) | copy-start | bytes 6148
  27.6 649.6 %all-reduce.12.cloned.1.call-start = ((), (), s32[]{:S(2)}) async-start(), calls=%async_computation.3 | async-start | bytes 1048576 | tf_op jit(solution)/shard_map/psum | solution.py:44
  387.9 458.1 %reduce-scatter.7.cloned.1.call-start = ((), (), s32[]{:S(2)}) async-start(), calls=%async_computation.5 | async-start | bytes 3784704
  395.9 807.2 %reduce-scatter.9.cloned.1.call-start = ((), (), s32[]{:S(2)}) async-start(), calls=%async_computation.6 | async-start | bytes 3784704
  1062.3 255.0 %copy-start.1 = (f32[64,2048]{1,0:T(8,128)S(1)}, f32[64,2048]{1,0:T(8,128)}, u32[]{:S(2)}) copy-start(f32[64,2048]{1,0:T(8,128)} %all-reduce.12.cloned.1.call-done) | copy-start | bytes 1572868
  1062.3 371.1 %all-gather.4.cloned.1.call-start = ((), (), s32[]{:S(2)}) async-start(), calls=%async_computation.4 | async-start | bytes 2162688 | tf_op jit(solution)/shard_map/all_gather | solution.py:54
  1318.0 119.6 %copy-start.2 = (f32[64,2048]{1,0:T(8,128)}, f32[64,2048]{1,0:T(8,128)S(1)}, u32[]{:S(2)}) copy-start(f32[64,2048]{1,0:T(8,128)S(1)} %fusion.30) | copy-start | bytes 1572868
Sparse Core Ops, SparseCore 0:
  27.8 291.3 all-reduce.9
  388.0 289.1 all-reduce.11
  679.6 166.3 reduce-scatter.6
  1062.4 140.6 reduce-scatter.8
  1305.2 128.1 all-gather.3
where the time goes:
time: 1490 us
  waiting for transfers between devices  989 us (66%)
  blocking collectives  376 us (25%)
  matrix products  51.1 us (3%)
  other arithmetic  48.3 us (3%)
    psum x2, waiting for transfers between devices, shards(): in_whole = lax.psum(in_image, 'dp')  567 us
    unnamed x7, waiting for transfers between devices  308 us
    psum x2, blocking collectives, shards(): gram_out = lax.psum(gram_of(out_owned), ('dp', 'mp'))  173 us
    all_gather x1, waiting for transfers between devices, shards(): basis_out = lax.all_gather(new_out, 'dp', axis=1, tiled=True)  115 us
    all_gather x1, blocking collectives, shards(): lax.all_gather(new_out.astype(jnp.bfloat16), 'dp', axis=1, tiled=True)  69.9 us
    psum x3, blocking collectives, shards(): in_coords, out_coords = lax.psum((in_coords, out_coords), 'mp')  61 us
    psum x1, blocking collectives, shards(): proj_in, proj_out = lax.psum((proj_in, proj_out), 'mp')  38.4 us
    psum x1, blocking collectives, shards(): gram_in = lax.psum(gram_of(in_whole), 'mp')  34.3 us
  transfers between devices with their start and end apart: 5, of which 5 were waited for; matrix products, arithmetic and copies ran while one was open for 2% of the time, Pallas kernels for 0%

commit v1 on v0

--- a/solution.py
+++ b/solution.py
@@ -51,7 +51,9 @@
             half_out = lax.all_gather(new_out.astype(jnp.bfloat16), "dp", axis=1, tiled=True)
         else:
             basis_in = new_in
-            basis_out = lax.all_gather(new_out, "dp", axis=1, tiled=True)
+            basis_out = jnp.concatenate(
+                lax.all_to_all(jnp.stack([new_out] * lax.axis_size("dp")), "dp", 0, 0), axis=1
+            )
     half_in = basis_in.astype(jnp.bfloat16)
     half_out = basis_out.astype(jnp.bfloat16)
     proj_in = coords_of(layer_inputs, half_in)

time: 1490 us -> 1380 us (0.926)
  waiting for transfers between devices: 989 us -> 887 us
  blocking collectives: 376 us -> 356 us
    all_gather x1 -> x0, waiting for transfers between devices: 115 us -> none  [shards(): basis_out = lax.all_gather(new_out, 'dp', axis=1, tiled=True)]
    psum x1, blocking collectives: 38.4 us -> 17.9 us  [shards(): proj_in, proj_out = lax.psum((proj_in, proj_out), 'mp')]
    unnamed x7 -> x6, waiting for transfers between devices: 308 us -> 307 us
where the time goes in v1:
time: 1380 us
  waiting for transfers between devices  887 us (64%)
  blocking collectives  356 us (26%)
  matrix products  50.5 us (4%)
  other arithmetic  48.3 us (4%)
  local copies, waits for them, and re-layouts  15 us (1%)
  between operations  14 us (1%)
    psum x2, waiting for transfers between devices, shards(): in_whole = lax.psum(in_image, 'dp')  567 us
    unnamed x6, waiting for transfers between devices  307 us
    psum x2, blocking collectives, shards(): gram_out = lax.psum(gram_of(out_owned), ('dp', 'mp'))  173 us
    all_gather x1, blocking collectives, shards(): lax.all_gather(new_out.astype(jnp.bfloat16), 'dp', axis=1, tiled=True)  69.9 us
    psum x3, blocking collectives, shards(): in_coords, out_coords = lax.psum((in_coords, out_coords), 'mp')  61 us
    psum x1, blocking collectives, shards(): gram_in = lax.psum(gram_of(in_whole), 'mp')  34.3 us
  transfers between devices with their start and end apart: 5, of which 5 were waited for; matrix products, arithmetic and copies ran while one was open for 2% of the time, Pallas kernels for 0%

profile of v1, /device:TPU:1, one launch (start us, length us, event | category | flops | bytes accessed | tf_op | source)
XLA Modules:
  0.0 1376.6 jit_solution(13789868344534174123)
XLA Ops:
  10.6 15.8 %all-reduce.13 = bf16[512,64]{0,1:T(8,128)(2,1)S(1)} all-reduce(f32[512,64]{0,1:T(8,128)S(1)} %convolution_bitcast_fusion.4), channel_id=1, replica_groups=mesh['dp'=32,'mp'=4] {'mp'}, use_global_device_ids=true, to_apply=%region_0.0 | all-reduce | flops 32768 | bytes 196608 | tf_op jit(solution)/shard_map/psum | solution.py:40
  27.7 6.0 fusion.2
  33.7 285.4 %all-reduce.10.cloned.1.call-done = f32[64,2048]{1,0:T(8,128)} async-done(((f32[64,2048]{1,0:T(8,128)}), f32[64,2048]{1,0:T(8,128)}) %all-reduce.10.cloned.1.call-update) | async-done | bytes 524304 | tf_op jit(solution)/shard_map/psum | solution.py:44
  320.9 34.3 %psum.86 = f32[64,64]{0,1:T(8,128)S(1)} all-reduce(f32[64,64]{0,1:T(8,128)S(1)} %fusion.42), channel_id=1, replica_groups=mesh['dp'=32,'mp'=4] {'mp'}, use_global_device_ids=true, to_apply=%region_2.0 | all-reduce | flops 4096 | bytes 32768 | tf_op jit(solution)/shard_map/psum | solution.py:45
  355.3 5.8 cholesky.74
  362.5 4.9 custom-call.10
  369.8 16.8 %all-reduce.14 = (bf16[512,64]{0,1:T(8,128)(2,1)S(1)}, bf16[512,64]{0,1:T(8,128)(2,1)S(1)}) all-reduce(f32[512,64]{0,1:T(8,128)S(1)} %fusion.2, f32[512,64]{0,1:T(8,128)S(1)} %convolution_bitcast_fusion.3), channel_id=1, replica_groups=mesh['dp'=32,'mp'=4] {'mp'}, use_global_device_ids=true, to_apply=%region_9.12 | all-reduce | flops 65536 | bytes 393216 | tf_op jit(solution)/shard_map/psum | solution.py:40
  388.0 7.9 convolution_bitcast_fusion.1
  395.9 281.3 %all-reduce.12.cloned.1.call-done = f32[64,2048]{1,0:T(8,128)} async-done(((f32[64,2048]{1,0:T(8,128)}), f32[64,2048]{1,0:T(8,128)}) %all-reduce.12.cloned.1.call-update) | async-done | bytes 524304 | tf_op jit(solution)/shard_map/psum | solution.py:44
  679.0 167.0 %reduce-scatter.7.cloned.1.call-done = f32[224,64]{1,0:T(8,128)} async-done(((f32[7168,64]{1,0:T(8,128)}), f32[224,64]{1,0:T(8,128)}) %reduce-scatter.7.cloned.1.call-update) | async-done | bytes 57360
  847.4 86.2 %psum.92 = f32[64,64]{0,1:T(8,128)S(1)} all-reduce(f32[64,64]{0,1:T(8,128)S(1)} %fusion.12), channel_id=1, replica_groups=mesh['dp'=32,'mp'=4] {'dp','mp'}, use_global_device_ids=true, to_apply=%region_11.14 | all-reduce | flops 4096 | bytes 32768 | tf_op jit(solution)/shard_map/psum | solution.py:46
  933.6 5.8 cholesky.96
  940.8 4.9 custom-call.12
  947.0 69.9 %all-gather = bf16[32,224,64]{1,2,0:T(8,128)(2,1)S(1)} all-gather(bf16[1,224,64]{1,2,0:T(8,128)(2,1)S(1)} %fusion.3), channel_id=1, replica_groups=mesh['dp'=32,'mp'=4] {'dp'}, dimensions={0}, use_global_device_ids=true | all-gather | bytes 946176 | tf_op jit(solution)/shard_map/all_gather | solution.py:51
  1020.2 5.7 fusion.1
  1026.0 28.4 %all-reduce.15 = (bf16[512,64]{0,1:T(8,128)(2,1)S(1)}, f32[64,64]{0,1:T(8,128)S(1)}) all-reduce(f32[512,64]{0,1:T(8,128)S(1)} %fusion.1, f32[64,64]{0,1:T(8,128)S(1)} %fusion.43), channel_id=1, replica_groups=mesh['dp'=32,'mp'=4] {'mp'}, use_global_device_ids=true, to_apply=%region_12.0 | all-reduce | flops 36864 | bytes 229376 | tf_op jit(solution)/shard_map/psum | solution.py:40
  1054.4 7.9 convolution_bitcast_fusion
  1062.3 140.0 %reduce-scatter.9.cloned.1.call-done = f32[224,64]{1,0:T(8,128)} async-done(((f32[7168,64]{1,0:T(8,128)}), f32[224,64]{1,0:T(8,128)}) %reduce-scatter.9.cloned.1.call-update) | async-done | bytes 57360
  1203.7 87.1 %psum.94 = f32[64,64]{0,1:T(8,128)S(1)} all-reduce(f32[64,64]{0,1:T(8,128)S(1)} %fusion.8), channel_id=1, replica_groups=mesh['dp'=32,'mp'=4] {'dp','mp'}, use_global_device_ids=true, to_apply=%region_14.18 | all-reduce | flops 4096 | bytes 32768 | tf_op jit(solution)/shard_map/psum | solution.py:46
  1290.9 5.8 cholesky.107
  1310.8 5.8 cholesky.85
  1324.3 13.5 all-to-all-done
  1345.3 6.0 fusion
  1351.3 17.9 %all-reduce.16 = (bf16[512,64]{0,1:T(8,128)(2,1)S(1)}, bf16[512,64]{0,1:T(8,128)(2,1)S(1)}) all-reduce(f32[512,64]{0,1:T(8,128)S(1)} %fusion, f32[512,64]{0,1:T(8,128)S(1)} %convolution_bitcast_fusion.2), channel_id=1, replica_groups=mesh['dp'=32,'mp'=4] {'mp'}, use_global_device_ids=true, to_apply=%region_15.19 | all-reduce | flops 65536 | bytes 393216 | tf_op jit(solution)/shard_map/psum | solution.py:63
  (61 shorter events, 52.3 us)
Async XLA Ops:
  7.2 1.6 copy-start
  7.2 312.0 %all-reduce.10.cloned.1.call-start = ((), (), s32[]{:S(2)}) async-start(), calls=%async_computation.3 | async-start | bytes 1048576 | tf_op jit(solution)/shard_map/psum | solution.py:44
  10.6 17.1 %copy-start.3 = (s32[512]{0:T(512)S(1)}, s32[512]{0:T(512)}, u32[]{:S(2)}) copy-start(s32[512]{0:T(512)} %param.12) | copy-start | bytes 6148
  27.6 649.6 %all-reduce.12.cloned.1.call-start = ((), (), s32[]{:S(2)}) async-start(), calls=%async_computation.4 | async-start | bytes 1048576 | tf_op jit(solution)/shard_map/psum | solution.py:44
  387.9 458.1 %reduce-scatter.7.cloned.1.call-start = ((), (), s32[]{:S(2)}) async-start(), calls=%async_computation.5 | async-start | bytes 3784704
  395.9 806.5 %reduce-scatter.9.cloned.1.call-start = ((), (), s32[]{:S(2)}) async-start(), calls=%async_computation.6 | async-start | bytes 3784704
  1305.8 17.1 %copy-start.1 = (f32[64,2048]{1,0:T(8,128)S(1)}, f32[64,2048]{1,0:T(8,128)}, u32[]{:S(2)}) copy-start(f32[64,2048]{1,0:T(8,128)} %all-reduce.12.cloned.1.call-done) | copy-start | bytes 1572868
  1305.8 32.0 %all-to-all-start = ((f32[32,64,224]{2,1,0:T(8,128)}), f32[32,64,224]{2,1,0:T(8,128)}, u32[]{:S(2)}, u32[]{:S(2)}) async-start(f32[32,64,224]{2,1,0:T(8,128)} %stack.2), calls=%async_computation | async-start | bytes 4194304 | tf_op jit(solution)/shard_map/all_to_all | solution.py:55
  1323.5 18.3 %copy-start.2 = (f32[64,2048]{1,0:T(8,128)}, f32[64,2048]{1,0:T(8,128)S(1)}, u32[]{:S(2)}) copy-start(f32[64,2048]{1,0:T(8,128)S(1)} %fusion.31) | copy-start | bytes 1572868
Sparse Core Ops, SparseCore 0:
  27.8 291.3 all-reduce.9
  388.0 289.1 all-reduce.11
  679.6 166.3 reduce-scatter.6
  1062.4 139.8 reduce-scatter.8
